TPU v7x, 512 devices: a whole 4x8x8 slice. The times are simulated.
512 devices in a mesh: gx: 64 (over z_lo, y, core), gy: 8 (over x, z_hi).
Axes of the slice: x: 4, y: 8, z: 8 (z_hi: 2, z_lo: 4; z = z_hi * 4 + z_lo), core: 2. Of those that a mesh axis runs over, the one named last changes fastest.
Arguments:
- forward_field: bfloat16 [2560, 128, 128], P('gy', 'gx'), may hold values from -6 to 6
- adjoint_field: bfloat16 [2560, 128, 128], P('gy', 'gx'), may hold values from -6 to 6
- row_scale: float32 [2560, 128], P('gy', 'gx'), may hold values from 0.5 to 2
- station_block: bfloat16 [2560, 2560], P('gy'), may hold values from -0.15625 to 0.15625
- jacobian_block: bfloat16 [2560, 2560], P('gy'), may hold values from -0.15625 to 0.15625
- shock_stations: int32 [16], replicated, may hold values from 0 to 127, as said below
Outputs:
- forward_image: bfloat16 [2560, 128, 128], P('gy', 'gx')
- adjoint_image: bfloat16 [2560, 128, 128], P('gy', 'gx')
Inputs may be any that keep to these rules, and one draw needn't show every extreme that they name: `shock_stations`: station indices, repeats possible; station 0 and station 128 - 1 are always listed.
All inputs are finite; a program needn't handle non-finite values.
Results may differ from a plain program's by a relative error of at most 0.013.
Values may be sent and summed in bfloat16 or wider, within the bound.
A program may use at most 64 MiB of HBM per device.

v0:
```python
import jax
import jax.numpy as jnp
from jax import lax
from jax.sharding import PartitionSpec as P

far_coeff = 1.0 / 12.0
near_coeff = 8.0 / 12.0
shock_gain = 0.5


def with_halo(block, sides, width):
    for axis, dim in sides:
        count = lax.axis_size(axis)
        forward = [(i, i + 1) for i in range(count - 1)]
        backward = [(target, source) for source, target in forward]
        low = lax.ppermute(
            lax.slice_in_dim(block, block.shape[dim] - width, None, axis=dim), axis, forward
        )
        high = lax.ppermute(lax.slice_in_dim(block, 0, width, axis=dim), axis, backward)
        block = jnp.concatenate([low, block, high], axis=dim)
    return block


def streamwise(ext, count):
    values = ext.astype(jnp.float32)
    return (
        far_coeff * values[:, 0:count]
        - near_coeff * values[:, 1 : 1 + count]
        + near_coeff * values[:, 3 : 3 + count]
        - far_coeff * values[:, 4 : 4 + count]
    )


def transposed(ext, count):
    values = ext.astype(jnp.float32)
    return (
        far_coeff * values[:, 4 : 4 + count]
        - near_coeff * values[:, 3 : 3 + count]
        + near_coeff * values[:, 1 : 1 + count]
        - far_coeff * values[:, 0:count]
    )


def second_diff(ext, count):
    values = ext.astype(jnp.float32)
    return values[:, 1 : 1 + count] - 2.0 * values[:, 2 : 2 + count] + values[:, 3 : 3 + count]


def left_dot(matrix, other):
    return lax.dot_general(
        matrix, other, (((0,), (0,)), ((), ())), preferred_element_type=jnp.float32
    )


def local(forward_field, adjoint_field, row_scale, station_block, jacobian_block, shock_stations):
    own_rows = forward_field.shape[0]
    count = forward_field.shape[1]
    width = forward_field.shape[2]
    flat = count * width
    total_rows = station_block.shape[1]
    first = lax.axis_index("gx") * count
    station_ids = first - 2 + jnp.arange(count + 4, dtype=jnp.int32)
    sigma_ext = jnp.any(station_ids[:, None] == shock_stations[None, :], axis=1).astype(jnp.float32)
    sigma_own = sigma_ext[2 : 2 + count]
    pencils = lax.all_gather(forward_field, "gy", axis=0, tiled=True)
    pencil_ext = with_halo(pencils, (("gx", 1),), 2)
    slope = streamwise(pencil_ext, count).astype(jnp.bfloat16)
    centre = pencil_ext[:, 2 : 2 + count].reshape(total_rows, flat)
    dense = jnp.dot(station_block, centre, preferred_element_type=jnp.float32)
    flux = jnp.dot(
        jacobian_block, slope.reshape(total_rows, flat), preferred_element_type=jnp.float32
    )
    own_ext = lax.dynamic_slice_in_dim(pencil_ext, lax.axis_index("gy") * own_rows, own_rows, 0)
    w_ext = with_halo(adjoint_field, (("gx", 1),), 2)
    forward_out = row_scale[:, :, None] * dense.reshape(own_rows, count, width) + flux.reshape(
        own_rows, count, width
    )
    forward_out = forward_out + shock_gain * sigma_own[None, :, None] * second_diff(own_ext, count)
    back = transposed(w_ext, count).astype(jnp.bfloat16).reshape(own_rows, flat)
    scaled = (
        (row_scale[:, :, None] * adjoint_field.astype(jnp.float32))
        .astype(jnp.bfloat16)
        .reshape(own_rows, flat)
    )
    summed = lax.psum_scatter(
        (left_dot(station_block, scaled) + left_dot(jacobian_block, back)).astype(jnp.bfloat16),
        "gy",
        scatter_dimension=0,
        tiled=True,
    ).astype(jnp.float32)
    weighted = sigma_ext[None, :, None] * w_ext.astype(jnp.float32)
    adjoint_out = summed.reshape(own_rows, count, width) + shock_gain * second_diff(weighted, count)
    return (forward_out.astype(jnp.bfloat16), adjoint_out.astype(jnp.bfloat16))


def solution(mesh):
    in_specs = (
        P("gy", "gx", None),
        P("gy", "gx", None),
        P("gy", "gx"),
        P("gy", None),
        P("gy", None),
        P(),
    )
    out_specs = (P("gy", "gx", None), P("gy", "gx", None))
    return jax.shard_map(local, mesh=mesh, in_specs=in_specs, out_specs=out_specs, check_vma=False)
```

profile of v0, /device:TPU:8, one launch (start us, length us, event | category | flops | bytes accessed | tf_op | source)
XLA Modules:
  0.0 205.7 jit_solution(1199272171501167596)
XLA Ops:
  7.2 1.7 copy.57
  9.0 0.9 copy.61
  10.0 1.9 collective-permute-start.2
  11.9 3.6 %collective-permute-start.3 = (bf16[320,2,128]{2,0,1:T(8,128)(2,1)S(1)}, bf16[320,2,128]{2,0,1:T(8,128)(2,1)S(1)}, u32[]{:S(2)}, u32[]{:S(2)}) collective-permute-start(bf16[320,2,128]{2,0,1:T(8,128)(2,1)S(1)} %copy.61), channel_id=1, source_target_pairs={{8,0},{16,8},{24,16},{32,24},{40,32},{48,40},{56,48},{64,56},{72,6... | collective-permute-start | bytes 491528 | tf_op jit(solution)/shard_map/ppermute | solution.py:19
  15.5 2.5 %fusion.41 = f32[256,2560]{1,0:T(8,128)S(1)} fusion(bf16[320,2560]{1,0:T(8,128)(2,1)} %param.9, f32[320,2]{0,1:T(2,128)} %param.8, bf16[320,2,128]{2,1,0:T(2,128)(2,1)} %param.7), kind=kOutput, calls=%fused_computation.45 | convolution fusion | flops 419676160 | bytes 4426240 | tf_op jit(solution)/shard_map/dot_general | solution.py:50
  18.4 0.9 fusion.1
  19.4 1.5 copy.71
  20.9 66.9 %all-gather.2.cloned.1.call-done = bf16[2560,2,128]{2,0,1:T(8,128)(2,1)} async-done(((bf16[320,2,128]{2,0,1:T(8,128)(2,1)}), bf16[2560,2,128]{2,0,1:T(8,128)(2,1)}) %all-gather.2.cloned.1.call-update) | async-done | bytes 1310736 | tf_op jit(solution)/shard_map/all_gather | solution.py:65
  87.8 2.0 collective-permute-start
  90.0 3.6 %collective-permute-start.1 = (bf16[2560,2,128]{2,0,1:T(8,128)(2,1)}, bf16[2560,2,128]{2,0,1:T(8,128)(2,1)}, u32[]{:S(2)}, u32[]{:S(2)}) collective-permute-start(bf16[2560,2,128]{2,0,1:T(8,128)(2,1)} %all-gather.2.cloned.1.call-done), channel_id=1, source_target_pairs={{8,0},{16,8},{24,16},{32,24},{40,32},{48,40},{56,48},{64,56},{72,6... | collective-permute-start | bytes 3932168 | tf_op jit(solution)/shard_map/ppermute | solution.py:19
  93.8 1.1 broadcast_multiply_fusion
  94.9 1.4 copy.58
  96.3 87.8 %reduce-scatter.4.cloned.1.call-done = bf16[320,256]{1,0:T(8,128)(2,1)} async-done(((bf16[2560,256]{1,0:T(8,128)(2,1)}), bf16[320,256]{1,0:T(8,128)(2,1)}) %reduce-scatter.4.cloned.1.call-update) | async-done | bytes 163856 | tf_op jit(solution)/shard_map/reduce_scatter | solution.py:85
  184.1 1.3 fusion.29
  185.5 0.8 copy.70
  186.3 1.4 constant_dynamic-update-slice_fusion.2
  187.9 1.5 constant_dynamic-update-slice_fusion
  189.9 1.0 dynamic-slice_convert_fusion
  191.0 1.8 fusion.3
  192.8 1.6 copy.59
  194.4 0.6 convolution_bitcast_fusion
  195.1 0.8 copy-done.2
  196.2 1.8 fusion.24
  198.0 0.8 copy.69
  (26 shorter events, 1.9 us)
Async XLA Ops:
  7.2 11.3 %copy-start = (bf16[320,2560]{1,0:T(8,128)(2,1)S(1)}, bf16[320,2560]{1,0:T(8,128)(2,1)}, u32[]{:S(2)}) copy-start(bf16[320,2560]{1,0:T(8,128)(2,1)} %param.10) | copy-start | bytes 4915204
  7.2 80.6 %all-gather.2.cloned.1.call-start = ((), (), s32[]{:S(2)}) async-start(), calls=%async_computation.1 | async-start | bytes 1474560 | tf_op jit(solution)/shard_map/all_gather | solution.py:65
  9.0 175.2 %reduce-scatter.4.cloned.1.call-start = ((), (), s32[]{:S(2)}) async-start(), calls=%async_computation.2 | async-start | bytes 1474560 | tf_op jit(solution)/shard_map/reduce_scatter | solution.py:85
  10.0 8.1 %collective-permute-start.2 = (bf16[320,2,128]{2,0,1:T(8,128)(2,1)S(1)}, bf16[320,2,128]{2,0,1:T(8,128)(2,1)S(1)}, u32[]{:S(2)}, u32[]{:S(2)}) collective-permute-start(bf16[320,2,128]{2,0,1:T(8,128)(2,1)S(1)} %copy.61), channel_id=1, source_target_pairs={{0,8},{8,16},{16,24},{24,32},{32,40},{40,48},{48,56},{56,64},{64,7... | collective-permute-start | bytes 491528 | tf_op jit(solution)/shard_map/ppermute | solution.py:16
  11.9 6.5 %collective-permute-start.3 = (bf16[320,2,128]{2,0,1:T(8,128)(2,1)S(1)}, bf16[320,2,128]{2,0,1:T(8,128)(2,1)S(1)}, u32[]{:S(2)}, u32[]{:S(2)}) collective-permute-start(bf16[320,2,128]{2,0,1:T(8,128)(2,1)S(1)} %copy.61), channel_id=1, source_target_pairs={{8,0},{16,8},{24,16},{32,24},{40,32},{48,40},{56,48},{64,56},{72,6... | collective-permute-start | bytes 491528 | tf_op jit(solution)/shard_map/ppermute | solution.py:19
  19.4 70.5 %copy-start.5 = (s32[16]{0:T(128)S(1)}, s32[16]{0:T(128)}, u32[]{:S(2)}) copy-start(s32[16]{0:T(128)} %param.11) | copy-start | bytes 196
  87.8 7.1 %copy-start.1 = (bf16[2560,2,128]{2,0,1:T(8,128)(2,1)S(1)}, bf16[2560,2,128]{2,0,1:T(8,128)(2,1)}, u32[]{:S(2)}) copy-start(bf16[2560,2,128]{2,0,1:T(8,128)(2,1)} %all-gather.2.cloned.1.call-done) | copy-start | bytes 3932164
  87.8 98.5 %collective-permute-start = (bf16[2560,2,128]{2,0,1:T(8,128)(2,1)}, bf16[2560,2,128]{2,0,1:T(8,128)(2,1)}, u32[]{:S(2)}, u32[]{:S(2)}) collective-permute-start(bf16[2560,2,128]{2,0,1:T(8,128)(2,1)} %all-gather.2.cloned.1.call-done), channel_id=1, source_target_pairs={{0,8},{8,16},{16,24},{24,32},{32,40},{40,48},{48,56},{56,64},{64,7... | collective-permute-start | bytes 3932168 | tf_op jit(solution)/shard_map/ppermute | solution.py:16
  90.0 97.9 %collective-permute-start.1 = (bf16[2560,2,128]{2,0,1:T(8,128)(2,1)}, bf16[2560,2,128]{2,0,1:T(8,128)(2,1)}, u32[]{:S(2)}, u32[]{:S(2)}) collective-permute-start(bf16[2560,2,128]{2,0,1:T(8,128)(2,1)} %all-gather.2.cloned.1.call-done), channel_id=1, source_target_pairs={{8,0},{16,8},{24,16},{32,24},{40,32},{48,40},{56,48},{64,56},{72,6... | collective-permute-start | bytes 3932168 | tf_op jit(solution)/shard_map/ppermute | solution.py:19
  194.4 1.4 copy-start.2
  194.4 1.8 copy-start.3
  194.4 1.8 copy-start.4
Sparse Core Ops, SparseCore 0:
  11.8 75.9 all-gather.1
  92.3 91.7 reduce-scatter.3
where the time goes:
time: 206 us
  waiting for transfers between devices  155 us (75%)
  between operations  14.2 us (7%)
  local copies, waits for them, and re-layouts  13.1 us (6%)
  starting transfers between devices  11.3 us (5%)
  other arithmetic  6.16 us (3%)
  matrix products  5.84 us (3%)
    reduce_scatter x1, waiting for transfers between devices, local(): lax.psum_scatter((left_dot(station_block, scaled) + left_dot(jacobian_blo...  87.8 us
    all_gather x1, waiting for transfers between devices, local(): pencils = lax.all_gather(forward_field, 'gy', axis=0, tiled=True)  66.9 us
    unnamed x19, local copies, waits for them, and re-layouts  8.54 us
    ppermute x2, starting transfers between devices, with_halo(): lax.ppermute(lax.slice_in_dim(block, 0, width, axis=dim), axis, backward)  7.28 us
  transfers between devices with their start and end apart: 6, of which 3 were waited for; matrix products, arithmetic and copies ran while one was open for 6% of the time, Pallas kernels for 0%

commit v1 on v0

--- a/solution.py
+++ b/solution.py
@@ -6,6 +6,13 @@
 far_coeff = 1.0 / 12.0
 near_coeff = 8.0 / 12.0
 shock_gain = 0.5
+
+
+def swapped_in(x, axis, dim):
+    devices = lax.axis_size(axis)
+    parts = jnp.stack([x for _ in range(devices)])
+    parts = lax.all_to_all(parts, axis, split_axis=0, concat_axis=0)
+    return jnp.concatenate(parts, axis=dim)
 
 
 def with_halo(block, sides, width):
@@ -62,7 +69,7 @@
     station_ids = first - 2 + jnp.arange(count + 4, dtype=jnp.int32)
     sigma_ext = jnp.any(station_ids[:, None] == shock_stations[None, :], axis=1).astype(jnp.float32)
     sigma_own = sigma_ext[2 : 2 + count]
-    pencils = lax.all_gather(forward_field, "gy", axis=0, tiled=True)
+    pencils = swapped_in(forward_field, "gy", 0)
     pencil_ext = with_halo(pencils, (("gx", 1),), 2)
     slope = streamwise(pencil_ext, count).astype(jnp.bfloat16)
     centre = pencil_ext[:, 2 : 2 + count].reshape(total_rows, flat)

time: 206 us -> 167 us (0.81)
  waiting for transfers between devices: 155 us -> 96.7 us
  starting transfers between devices: 11.3 us -> 24 us
  other arithmetic: 6.16 us -> 11.2 us
    all_gather x1 -> x0, waiting for transfers between devices: 66.9 us -> none  [local(): pencils = lax.all_gather(forward_field, 'gy', axis=0, tiled=True)]
    all_to_all x0 -> x1, waiting for transfers between devices: none -> 14.8 us  [swapped_in(): parts = lax.all_to_all(parts, axis, split_axis=0, concat_axis=0)]
    all_to_all x0 -> x1, starting transfers between devices: none -> 12.9 us  [swapped_in(): parts = lax.all_to_all(parts, axis, split_axis=0, concat_axis=0)]
    reduce_scatter x1, waiting for transfers between devices: 87.8 us -> 81.9 us  [local(): lax.psum_scatter((left_dot(station_block, scaled) + left_dot(jacobian_blo...]
    concatenate x0 -> x1, other arithmetic: none -> 3.77 us  [with_halo(): block = jnp.concatenate([low, block, high], axis=dim)]
    another operation x0 -> x1, local copies, waits for them, and re-layouts: none -> 2.65 us  [swapped_in(): parts = jnp.stack([x for _ in range(devices)])]
    dot_general x0 -> x1, local copies, waits for them, and re-layouts: none -> 2.52 us  [local(): dense = jnp.dot(station_block, centre, preferred_element_type=jnp.float32)]
    unnamed x19, local copies, waits for them, and re-layouts: 8.54 us -> 6.43 us
  transfers between devices with their start and end apart: 6 -> 6, of which waited for: 3 -> 2; matrix products, arithmetic and copies ran while one was open for 6% -> 12% of each run, Pallas kernels for 0% -> 0%
where the time goes in v1:
time: 167 us; the launch traced here: 166 us
  waiting for transfers between devices  96.7 us (58%)
  starting transfers between devices  24 us (14%)
  local copies, waits for them, and re-layouts  14.5 us (9%)
  between operations  14.2 us (9%)
  other arithmetic  11.2 us (7%)
  matrix products  5.59 us (3%)
    reduce_scatter x1, waiting for transfers between devices, local(): lax.psum_scatter((left_dot(station_block, scaled) + left_dot(jacobian_blo...  81.9 us
    all_to_all x1, waiting for transfers between devices, swapped_in(): parts = lax.all_to_all(parts, axis, split_axis=0, concat_axis=0)  14.8 us
    all_to_all x1, starting transfers between devices, swapped_in(): parts = lax.all_to_all(parts, axis, split_axis=0, concat_axis=0)  12.9 us
    ppermute x2, starting transfers between devices, with_halo(): lax.ppermute(lax.slice_in_dim(block, 0, width, axis=dim), axis, backward)  7.29 us
    unnamed x19, local copies, waits for them, and re-layouts  6.43 us
    dot_general x2, matrix products, left_dot(): lax.dot_general(matrix, other, (((0,), (0,)), ((), ())), preferred_elemen...  4.35 us
    ppermute x2, starting transfers between devices, with_halo(): lax.ppermute(lax.slice_in_dim(block, block.shape[dim] - width, None, axis...  3.83 us
    concatenate x1, other arithmetic, with_halo(): block = jnp.concatenate([low, block, high], axis=dim)  3.77 us
  transfers between devices with their start and end apart: 6, of which 2 were waited for; matrix products, arithmetic and copies ran while one was open for 12% of the time, Pallas kernels for 0%

profile of v1, /device:TPU:8, one launch (start us, length us, event | category | flops | bytes accessed | tf_op | source)
XLA Modules:
  0.0 166.3 jit_solution(9959690324860029389)
XLA Ops:
  7.2 1.1 copy.62
  8.2 1.9 %collective-permute-start.2 = (bf16[320,2,128]{2,0,1:T(8,128)(2,1)S(1)}, bf16[320,2,128]{2,0,1:T(8,128)(2,1)S(1)}, u32[]{:S(2)}, u32[]{:S(2)}) collective-permute-start(bf16[320,2,128]{2,0,1:T(8,128)(2,1)S(1)} %copy.62), channel_id=1, source_target_pairs={{0,8},{8,16},{16,24},{24,32},{32,40},{40,48},{48,56},{56,64},{64,7... | collective-permute-start | bytes 491528 | tf_op jit(solution)/shard_map/ppermute | solution.py:23
  10.2 3.6 %collective-permute-start.3 = (bf16[320,2,128]{2,0,1:T(8,128)(2,1)S(1)}, bf16[320,2,128]{2,0,1:T(8,128)(2,1)}, u32[]{:S(2)}, u32[]{:S(2)}) collective-permute-start(bf16[320,2,128]{2,0,1:T(8,128)(2,1)S(1)} %copy.62), channel_id=1, source_target_pairs={{8,0},{16,8},{24,16},{32,24},{40,32},{48,40},{56,48},{64,56},{72,6... | collective-permute-start | bytes 491528 | tf_op jit(solution)/shard_map/ppermute | solution.py:26
  13.8 2.6 %stack.2 = bf16[8,320,2,128]{3,2,1,0:T(2,128)(2,1)} broadcast(bf16[320,2,128]{2,1,0:T(2,128)(2,1)} %param.6), dimensions={1,2,3} | broadcast | bytes 1474560 | tf_op jit(solution)/shard_map/stack | solution.py:13
  16.5 12.9 %all-to-all-start = ((bf16[8,320,2,128]{3,2,1,0:T(2,128)(2,1)}), bf16[8,320,2,128]{3,2,1,0:T(2,128)(2,1)S(1)}, u32[]{:S(2)}, u32[]{:S(2)}) async-start(bf16[8,320,2,128]{3,2,1,0:T(2,128)(2,1)} %stack.2), calls=%async_computation | async-start | bytes 2621440 | tf_op jit(solution)/shard_map/all_to_all | solution.py:14
  29.4 2.4 %fusion.32 = f32[256,2560]{1,0:T(8,128)S(1)} fusion(bf16[320,2560]{1,0:T(8,128)(2,1)} %param.9, f32[320,2]{0,1:T(2,128)S(1)} %copy-done.5, bf16[320,2,128]{2,1,0:T(2,128)(2,1)S(1)} %copy-done.4), kind=kOutput, calls=%fused_computation.46 | convolution fusion | flops 419676160 | bytes 4426240 | tf_op jit(solution)/shard_map/dot_general | solution.py:57
  31.8 1.0 maximum_convert_fusion
  32.8 2.0 %fusion.1 = bf16[2560,256]{0,1:T(8,128)(2,1)} fusion(f32[256,2560]{1,0:T(8,128)S(1)} %fusion.32, bf16[320,2560]{1,0:T(8,128)(2,1)S(1)} %copy-done, f32[320,6,128]{2,0,1:T(8,128)S(1)} %maximum_convert_fusion), kind=kOutput, calls=%fused_computation.3 | convolution fusion | flops 421396480 | bytes 6881280 | tf_op jit(solution)/shard_map/dot_general | solution.py:57
  34.8 2.4 %copy.72 = bf16[2560,256]{1,0:T(8,128)(2,1)} copy(bf16[2560,256]{0,1:T(8,128)(2,1)} %fusion.1) | data formatting | bytes 2621440
  37.3 14.8 %all-to-all-done = bf16[8,320,2,128]{3,2,1,0:T(2,128)(2,1)S(1)} async-done(((bf16[8,320,2,128]{3,2,1,0:T(2,128)(2,1)}), bf16[8,320,2,128]{3,2,1,0:T(2,128)(2,1)S(1)}, u32[]{:S(2)}, u32[]{:S(2)}) %all-to-all-start) | async-done | bytes 1310752 | tf_op jit(solution)/shard_map/all_to_all | solution.py:14
  52.1 1.4 copy.59
  53.4 1.9 %collective-permute-start = (bf16[2560,2,128]{2,0,1:T(8,128)(2,1)}, bf16[2560,2,128]{2,0,1:T(8,128)(2,1)}, u32[]{:S(2)}, u32[]{:S(2)}) collective-permute-start(bf16[2560,2,128]{2,0,1:T(8,128)(2,1)} %bitcast.3), channel_id=1, source_target_pairs={{0,8},{8,16},{16,24},{24,32},{32,40},{40,48},{48,56},{56,64},{64,7... | collective-permute-start | bytes 3932168 | tf_op jit(solution)/shard_map/ppermute | solution.py:23
  55.4 3.6 %collective-permute-start.1 = (bf16[2560,2,128]{2,0,1:T(8,128)(2,1)}, bf16[2560,2,128]{2,0,1:T(8,128)(2,1)}, u32[]{:S(2)}, u32[]{:S(2)}) collective-permute-start(bf16[2560,2,128]{2,0,1:T(8,128)(2,1)} %bitcast.3), channel_id=1, source_target_pairs={{8,0},{16,8},{24,16},{32,24},{40,32},{48,40},{56,48},{64,56},{72,6... | collective-permute-start | bytes 3932168 | tf_op jit(solution)/shard_map/ppermute | solution.py:26
  59.3 2.0 %broadcast_multiply_fusion = f32[320,6,128]{2,0,1:T(8,128)} fusion(f32[6]{0:T(128)S(1)} %convert_element_type.44, bf16[320,2,128]{2,0,1:T(8,128)(2,1)} %collective-permute-done.3, bf16[320,2,128]{2,0,1:T(8,128)(2,1)S(1)} %copy.62, bf16[320,2,128]{2,0,1:T(8,128)(2,1)S(1)} %collective-permute-done.2), kind=kLoop, calls=%fused_computation.21 | loop fusion | flops 983040 | bytes 1474584 | tf_op jit(solution)/shard_map/mul | solution.py:98
  61.3 1.2 copy.93
  62.5 2.5 %copy.58 = bf16[256,2560]{1,0:T(8,128)(2,1)} copy(bf16[256,2560]{0,1:T(8,128)(2,1)} %bitcast.58) | data formatting | bytes 2621440 | tf_op jit(solution)/shard_map/dot_general | solution.py:76
  65.1 81.9 %reduce-scatter.4.cloned.1.call-done = bf16[320,256]{1,0:T(8,128)(2,1)} async-done(((bf16[2560,256]{1,0:T(8,128)(2,1)}), bf16[320,256]{1,0:T(8,128)(2,1)}) %reduce-scatter.4.cloned.1.call-update) | async-done | bytes 163856 | tf_op jit(solution)/shard_map/reduce_scatter | solution.py:92
  147.0 1.0 fusion.20
  148.0 0.8 copy.71
  148.8 3.8 %pad_maximum_fusion = (bf16[2560,6,128]{2,0,1:T(8,128)(2,1)}, f32[2560,6,128]{2,0,1:T(8,128)S(1)}) fusion(bf16[2560,2,128]{2,0,1:T(8,128)(2,1)} %collective-permute-done.1, bf16[2560,2,128]{2,0,1:T(8,128)(2,1)} %bitcast.3, bf16[2560,2,128]{2,0,1:T(8,128)(2,1)} %collective-permute-done), kind=kLoop, calls=%fused_computation.1 | loop fusion | flops 5898240 | bytes 15728640 | tf_op jit(solution)/shard_map/concatenate | solution.py:27
  152.6 1.8 %fusion.3 = bf16[2560,2,128]{2,0,1:T(8,128)(2,1)} fusion(f32[2560,6,128]{2,0,1:T(8,128)S(1)} %get-tuple-element.13), kind=kLoop, calls=%fused_computation.6 | loop fusion | flops 5242880 | bytes 11796480 | tf_op jit(solution)/shard_map/convert_element_type | solution.py:74
  154.4 1.6 copy.60
  156.7 1.3 dynamic-slice_convert_fusion
  158.7 0.8 copy.70
  (26 shorter events, 1.6 us)
Async XLA Ops:
  7.2 25.7 %copy-start = (bf16[320,2560]{1,0:T(8,128)(2,1)S(1)}, bf16[320,2560]{1,0:T(8,128)(2,1)}, u32[]{:S(2)}) copy-start(bf16[320,2560]{1,0:T(8,128)(2,1)} %param.10) | copy-start | bytes 4915204
  8.2 23.6 %collective-permute-start.2 = (bf16[320,2,128]{2,0,1:T(8,128)(2,1)S(1)}, bf16[320,2,128]{2,0,1:T(8,128)(2,1)S(1)}, u32[]{:S(2)}, u32[]{:S(2)}) collective-permute-start(bf16[320,2,128]{2,0,1:T(8,128)(2,1)S(1)} %copy.62), channel_id=1, source_target_pairs={{0,8},{8,16},{16,24},{24,32},{32,40},{40,48},{48,56},{56,64},{64,7... | collective-permute-start | bytes 491528 | tf_op jit(solution)/shard_map/ppermute | solution.py:23
  10.2 21.6 %collective-permute-start.3 = (bf16[320,2,128]{2,0,1:T(8,128)(2,1)S(1)}, bf16[320,2,128]{2,0,1:T(8,128)(2,1)}, u32[]{:S(2)}, u32[]{:S(2)}) collective-permute-start(bf16[320,2,128]{2,0,1:T(8,128)(2,1)S(1)} %copy.62), channel_id=1, source_target_pairs={{8,0},{16,8},{24,16},{32,24},{40,32},{48,40},{56,48},{64,56},{72,6... | collective-permute-start | bytes 491528 | tf_op jit(solution)/shard_map/ppermute | solution.py:26
  16.5 12.9 %copy-start.4 = (bf16[320,2,128]{2,1,0:T(2,128)(2,1)S(1)}, bf16[320,2,128]{2,1,0:T(2,128)(2,1)}, u32[]{:S(2)}) copy-start(bf16[320,2,128]{2,1,0:T(2,128)(2,1)} %param.7) | copy-start | bytes 491524
  16.5 12.9 %copy-start.5 = (f32[320,2]{0,1:T(2,128)S(1)}, f32[320,2]{0,1:T(2,128)}, u32[]{:S(2)}) copy-start(f32[320,2]{0,1:T(2,128)} %param.8) | copy-start | bytes 7684
  16.5 35.6 %all-to-all-start = ((bf16[8,320,2,128]{3,2,1,0:T(2,128)(2,1)}), bf16[8,320,2,128]{3,2,1,0:T(2,128)(2,1)S(1)}, u32[]{:S(2)}, u32[]{:S(2)}) async-start(bf16[8,320,2,128]{3,2,1,0:T(2,128)(2,1)} %stack.2), calls=%async_computation | async-start | bytes 2621440 | tf_op jit(solution)/shard_map/all_to_all | solution.py:14
  29.4 117.6 %reduce-scatter.4.cloned.1.call-start = ((), (), s32[]{:S(2)}) async-start(), calls=%async_computation.2 | async-start | bytes 1474560 | tf_op jit(solution)/shard_map/reduce_scatter | solution.py:92
  37.3 21.8 %copy-start.6 = (s32[16]{0:T(128)S(1)}, s32[16]{0:T(128)}, u32[]{:S(2)}) copy-start(s32[16]{0:T(128)} %param.11) | copy-start | bytes 196
  53.4 95.4 %collective-permute-start = (bf16[2560,2,128]{2,0,1:T(8,128)(2,1)}, bf16[2560,2,128]{2,0,1:T(8,128)(2,1)}, u32[]{:S(2)}, u32[]{:S(2)}) collective-permute-start(bf16[2560,2,128]{2,0,1:T(8,128)(2,1)} %bitcast.3), channel_id=1, source_target_pairs={{0,8},{8,16},{16,24},{24,32},{32,40},{40,48},{48,56},{56,64},{64,7... | collective-permute-start | bytes 3932168 | tf_op jit(solution)/shard_map/ppermute | solution.py:23
  55.4 93.4 %collective-permute-start.1 = (bf16[2560,2,128]{2,0,1:T(8,128)(2,1)}, bf16[2560,2,128]{2,0,1:T(8,128)(2,1)}, u32[]{:S(2)}, u32[]{:S(2)}) collective-permute-start(bf16[2560,2,128]{2,0,1:T(8,128)(2,1)} %bitcast.3), channel_id=1, source_target_pairs={{8,0},{16,8},{24,16},{32,24},{40,32},{48,40},{56,48},{64,56},{72,6... | collective-permute-start | bytes 3932168 | tf_op jit(solution)/shard_map/ppermute | solution.py:26
  62.5 84.4 %copy-start.1 = (f32[320,6,128]{2,0,1:T(8,128)S(1)}, f32[320,6,128]{2,0,1:T(8,128)}, u32[]{:S(2)}) copy-start(f32[320,6,128]{2,0,1:T(8,128)} %broadcast_multiply_fusion) | copy-start | bytes 2949124
  156.0 2.0 %copy-start.2 = (bf16[320,2560]{1,0:T(8,128)(2,1)S(1)}, bf16[320,2560]{1,0:T(8,128)(2,1)}, u32[]{:S(2)}) copy-start(bf16[320,2560]{1,0:T(8,128)(2,1)} %param.9) | copy-start | bytes 4915204
  156.0 2.0 %copy-start.3 = (bf16[256,2560]{1,0:T(8,128)(2,1)S(1)}, bf16[256,2560]{1,0:T(8,128)(2,1)}, u32[]{:S(2)}) copy-start(bf16[256,2560]{1,0:T(8,128)(2,1)} %copy.58) | copy-start | bytes 3932164
Sparse Core Ops, SparseCore 0:
  37.4 109.5 reduce-scatter.3
